TPU v7x, 512 devices: a whole 4x8x8 slice. The times are simulated.
512 devices in a mesh: mode: 8 (over x, core), ax: 32 (over y, z_hi), rad: 2 (over z_lo).
Axes of the slice: x: 4, y: 8, z: 8 (z_hi: 4, z_lo: 2; z = z_hi * 2 + z_lo), core: 2. Of those that a mesh axis runs over, the one named last changes fastest.
Arguments:
- adjoint: float32 [5, 256, 128, 256], P(None, 'mode', 'ax', 'rad'), may hold values from -6 to 6
- state: float32 [5, 256, 128, 256], P(None, 'mode', 'ax', 'rad'), may hold values from -6 to 6
- wake: float32 [256, 128, 256], P('mode', 'ax', 'rad'), may hold values from 0.2 to 1.5
- jac_axial: float32 [5, 5], replicated, may hold values from -2.5 to 2.5
- jac_radial: float32 [5, 5], replicated, may hold values from -2.5 to 2.5
- jac_swirl: float32 [5, 5], replicated, may hold values from -2.5 to 2.5
- wake_coupling: float32 [5, 5], replicated, may hold values from -2.5 to 2.5
Outputs:
- adjoint_in: float32 [5, 256, 128, 256], P(None, 'mode', 'ax', 'rad')
- wake_grad: float32 [256, 128, 256], P('mode', 'ax', 'rad')
All inputs are finite; a program needn't handle non-finite values.
Results may differ from a plain program's by a relative error of at most 0.000098.
Values sent between devices are 32-bit elements; how exact they have to be, the bound alone decides.
A program may use at most 64 MiB of HBM per device.

v0:
```python
import math

import jax
import jax.numpy as jnp
from jax import lax
from jax.sharding import PartitionSpec as P

exact_prec = lax.Precision.HIGHEST


def with_halo(x, sides, width):
    edges = {}
    for axis, dim in sides:
        size, length = (lax.axis_size(axis), x.shape[dim])
        up = [(i, (i + 1) % size) for i in range(size - 1)]
        last = lax.slice_in_dim(x, length - width, length, axis=dim)
        first = lax.slice_in_dim(x, 0, width, axis=dim)
        edges[dim] = (
            lax.ppermute(last, axis, up),
            lax.ppermute(first, axis, [(b, a) for a, b in up]),
        )
    done = []
    for _, dim in sides:
        low, high = edges[dim]
        around = [(width, width) if d in done else (0, 0) for d in range(x.ndim)]
        x = jnp.concatenate([jnp.pad(low, around), x, jnp.pad(high, around)], axis=dim)
        done.append(dim)
    return x


def in_one_piece(arrays, axis, split_dim, concat_dim, along):
    widths = [a.shape[along] for a in arrays]
    both = jnp.concatenate(arrays, axis=along)
    filled = lax.all_to_all(both, axis, split_axis=split_dim, concat_axis=concat_dim, tiled=True)
    return tuple(jnp.split(filled, [sum(widths[:k]) for k in range(1, len(widths))], axis=along))


def fourier_basis(mode_count):
    angle_idx = jnp.arange(mode_count, dtype=jnp.int32)[:, None]
    coef_idx = jnp.arange(mode_count, dtype=jnp.int32)[None, :]
    orders = coef_idx // 2
    phases = (orders * angle_idx % mode_count).astype(jnp.float32) * jnp.float32(
        2.0 * math.pi / mode_count
    )
    scale_two = jnp.float32(math.sqrt(2.0 / mode_count))
    scale_one = jnp.float32(1.0 / math.sqrt(mode_count))
    table = jnp.where(coef_idx % 2 == 0, scale_two * jnp.cos(phases), scale_two * jnp.sin(phases))
    table = jnp.where(coef_idx == 0, scale_one, table)
    signs = jnp.where(angle_idx % 2 == 0, scale_one, -scale_one)
    table = jnp.where(coef_idx == 1, signs, table)
    return table


def rotate(field, first_order, mode_count):
    fields, modes_here, cells_ax, cells_rad = field.shape
    paired = field.reshape(fields, modes_here // 2, 2, cells_ax, cells_rad)
    orders = (first_order + jnp.arange(modes_here // 2, dtype=jnp.int32)).astype(
        jnp.float32
    ) / jnp.float32(mode_count // 2)
    orders = orders[None, :, None, None]
    turned = jnp.stack([orders * paired[:, :, 1], -orders * paired[:, :, 0]], axis=2)
    return turned.reshape(fields, modes_here, cells_ax, cells_rad)


def body(adjoint, state, wake, jac_axial, jac_radial, jac_swirl, wake_coupling):
    fields, modes_here, cells_ax, cells_rad = adjoint.shape
    mode_groups = lax.axis_size("mode")
    mode_count = modes_here * mode_groups
    points = cells_ax * cells_rad
    padded = with_halo(adjoint, (("ax", 2), ("rad", 3)), 1)
    axial_diff = 0.5 * (padded[:, :, 2:, 1:-1] - padded[:, :, :-2, 1:-1])
    radial_diff = 0.5 * (padded[:, :, 1:-1, 2:] - padded[:, :, 1:-1, :-2])
    rad_first = lax.axis_index("rad") * cells_rad
    radial_total = cells_rad * lax.axis_size("rad")
    radius = 0.5 + (
        (rad_first + jnp.arange(cells_rad, dtype=jnp.int32)).astype(jnp.float32) + 0.5
    ) / jnp.float32(2.0 * radial_total)
    swirl_rate = 0.25 / radius
    turned = rotate(adjoint, lax.axis_index("mode") * (modes_here // 2), mode_count) * swirl_rate
    transport = jnp.einsum("ef,ekxr->fkxr", jac_axial, axial_diff, precision=exact_prec)
    transport = transport + jnp.einsum(
        "ef,ekxr->fkxr", jac_radial, radial_diff, precision=exact_prec
    )
    transport = transport + jnp.einsum("ef,ekxr->fkxr", jac_swirl, turned, precision=exact_prec)
    coupled = jnp.einsum("fe,ekxr->fkxr", wake_coupling, state, precision=exact_prec)
    flat_adj = adjoint.reshape(fields, modes_here, points)
    flat_cpl = coupled.reshape(fields, modes_here, points)
    flat_wake = wake.reshape(1, modes_here, points)
    basis_table = fourier_basis(mode_count)
    adj_recv, cpl_recv, wake_recv = in_one_piece((flat_adj, flat_cpl, flat_wake), "mode", 2, 1, 0)
    adj_angle = jnp.einsum("tk,fkp->ftp", basis_table, adj_recv, precision=exact_prec)
    cpl_angle = jnp.einsum("tk,fkp->ftp", basis_table, cpl_recv, precision=exact_prec)
    grad_here = -jnp.sum(adj_angle * cpl_angle, axis=0, keepdims=True)
    returned = jnp.einsum("tk,ftp->fkp", basis_table, wake_recv * adj_angle, precision=exact_prec)
    back_home, grad_home = in_one_piece((returned, grad_here), "mode", 1, 2, 0)
    back_field = back_home.reshape(fields, modes_here, cells_ax, cells_rad)
    wake_grad = grad_home.reshape(modes_here, cells_ax, cells_rad)
    adjoint_in = (
        adjoint
        + transport
        - jnp.einsum("ef,ekxr->fkxr", wake_coupling, back_field, precision=exact_prec)
    )
    return (adjoint_in, wake_grad)


def solution(mesh):
    return jax.shard_map(
        body,
        mesh=mesh,
        in_specs=(
            P(None, "mode", "ax", "rad"),
            P(None, "mode", "ax", "rad"),
            P("mode", "ax", "rad"),
            P(),
            P(),
            P(),
            P(),
        ),
        out_specs=(P(None, "mode", "ax", "rad"), P("mode", "ax", "rad")),
        check_vma=False,
    )
```

profile of v0, /device:TPU:32, one launch (start us, length us, event | category | flops | bytes accessed | tf_op | source)
XLA Modules:
  0.0 89.0 jit_solution(2650055401326204937)
XLA Ops:
  0.6 1.0 %copy-done = f32[5,32,4,128]{3,2,1,0:T(4,128)S(1)} copy-done((f32[5,32,4,128]{3,2,1,0:T(4,128)S(1)}, f32[5,32,4,128]{3,2,1,0:T(4,128)}, u32[]{:S(2)}) %copy-start) | copy-done | bytes 327704
  1.6 1.4 %fusion.6 = f32[5,32,4,128]{3,0,2,1:T(8,128)S(1)} fusion(f32[5,32,4,128]{3,2,1,0:T(4,128)S(1)} %copy-done, f32[5,5]{1,0:T(8,128)} %param.13), kind=kOutput, calls=%fused_computation.14 | convolution fusion | flops 4915200 | bytes 655460 | tf_op jit(solution)/shard_map/fe,ekxr->fkxr/dot_general | solution.py:85
  3.3 1.1 %reshape.146 = f32[5,32,512]{2,1,0:T(8,128)S(1)} reshape(f32[5,32,4,128]{3,2,1,0:T(4,128)} %param.7) | data formatting | bytes 655360 | tf_op jit(solution)/shard_map/reshape | solution.py:86
  4.4 0.9 reshape.148
  5.3 3.6 %copy.70 = f32[11,32,512]{1,0,2:T(8,128)} copy(f32[11,32,512]{2,1,0:T(8,128)S(1)} %pad_maximum_fusion) | data formatting | bytes 1441792 | tf_op jit(solution)/shard_map/concatenate | solution.py:33
  9.0 4.5 %reshape.157 = f32[8,1,22528]{2,1,0:T(1,128)} reshape(f32[512,11,32]{2,1,0:T(8,128)} %bitcast.66) | data formatting | bytes 1441792
  13.4 4.4 %all-to-all-start = ((f32[8,1,22528]{2,1,0:T(1,128)}), f32[8,1,22528]{2,1,0:T(1,128)S(1)}, u32[]{:S(2)}, u32[]{:S(2)}) async-start(f32[8,1,22528]{2,1,0:T(1,128)} %reshape.157), calls=%async_computation | async-start | bytes 1441792 | tf_op jit(solution)/shard_map/all_to_all | solution.py:34
  17.9 0.9 %fusion.55 = (f32[5,32,4,1]{3,2,1,0:T(4,128)}, f32[5,32,4,1]{3,2,1,0:T(4,128)S(1)}) fusion(f32[5,32,4,128]{3,2,1,0:T(4,128)S(1)} %copy-done.1), kind=kLoop, calls=%fused_computation.92 | loop fusion | bytes 10240 | tf_op jit(solution)/shard_map/slice | solution.py:17
  18.8 1.3 %collective-permute-start.2 = (f32[5,32,4,1]{3,2,1,0:T(4,128)}, f32[5,32,4,1]{3,2,1,0:T(4,128)S(1)}, u32[]{:S(2)}, u32[]{:S(2)}) collective-permute-start(f32[5,32,4,1]{3,2,1,0:T(4,128)} %get-tuple-element.16), channel_id=1, source_target_pairs={{1,0},{3,2},{5,4},{7,6},{9,8},{11,10},{13,12},{15,14},{17,16},{19,... | collective-permute-start | bytes 7688 | tf_op jit(solution)/shard_map/ppermute | solution.py:20
  20.1 5.3 %collective-permute-start.3 = (f32[5,32,4,1]{3,2,1,0:T(4,128)S(1)}, f32[5,32,4,1]{3,2,1,0:T(4,128)}, u32[]{:S(2)}, u32[]{:S(2)}) collective-permute-start(f32[5,32,4,1]{3,2,1,0:T(4,128)S(1)} %get-tuple-element.17), channel_id=1, source_target_pairs={{0,1},{2,3},{4,5},{6,7},{8,9},{10,11},{12,13},{14,15},{16,17},{18,... | collective-permute-start | bytes 7688 | tf_op jit(solution)/shard_map/ppermute | solution.py:19
  25.5 10.8 %collective-permute-start = (f32[5,32,1,128]{3,2,1,0:T(1,128)S(1)}, f32[5,32,1,128]{3,2,1,0:T(1,128)S(1)}, u32[]{:S(2)}, u32[]{:S(2)}) collective-permute-start(f32[5,32,1,128]{3,2,1,0:T(1,128)S(1)} %get-tuple-element.18), channel_id=1, source_target_pairs={{2,0},{4,2},{6,4},{8,6},{10,8},{12,10},{14,12},{16,14},{18,16},{20... | collective-permute-start | bytes 245768 | tf_op jit(solution)/shard_map/ppermute | solution.py:20
  36.3 1.9 %collective-permute-start.1 = (f32[5,32,1,128]{3,2,1,0:T(1,128)S(1)}, f32[5,32,1,128]{3,2,1,0:T(1,128)S(1)}, u32[]{:S(2)}, u32[]{:S(2)}) collective-permute-start(f32[5,32,1,128]{3,2,1,0:T(1,128)S(1)} %get-tuple-element.19), channel_id=1, source_target_pairs={{0,2},{2,4},{4,6},{6,8},{8,10},{10,12},{12,14},{14,16},{16,18},{18... | collective-permute-start | bytes 245768 | tf_op jit(solution)/shard_map/ppermute | solution.py:19
  38.9 8.0 %collective-permute-done.1 = f32[5,32,1,128]{3,2,1,0:T(1,128)S(1)} collective-permute-done((f32[5,32,1,128]{3,2,1,0:T(1,128)S(1)}, f32[5,32,1,128]{3,2,1,0:T(1,128)S(1)}, u32[]{:S(2)}, u32[]{:S(2)}) %collective-permute-start.1) | collective-permute-done | bytes 81952 | tf_op jit(solution)/shard_map/ppermute | solution.py:19
  46.9 2.5 %fusion.13 = (f32[5,32,4,128]{3,2,1,0:T(4,128)S(1)}, f32[5,32,4,128]{3,2,1,0:T(4,128)S(1)}) fusion(f32[5,32,4,1]{3,2,1,0:T(4,128)} %collective-permute-done.3, f32[5,32,1,128]{3,2,1,0:T(1,128)S(1)} %collective-permute-done, f32[5,32,4,128]{3,2,1,0:T(4,128)S(1)} %copy-done.1, f32[5,32,1,128]{3,2,1,0:T(1,128)S(1)} %collective-permute-done.1, ...), kind=kLoop, calls=%fused_computation.26 | loop fusion | flops 1474560 | bytes 1152000 | tf_op jit(solution)/shard_map/mul | solution.py:72
  49.3 0.8 fusion.9
  50.1 0.5 broadcast.226
  50.6 2.4 %reduce = f32[8,22528]{1,0:T(8,128)S(1)} reduce(f32[8,1,22528]{2,1,0:T(1,128)S(1)} %all-to-all-done, f32[]{:T(128)} %broadcast.226), dimensions={1}, to_apply=%all_to_all.22.reduce_sub_computation | reduce | bytes 1441796 | tf_op jit(solution)/shard_map/all_to_all | solution.py:34
  53.0 3.5 %reshape.158 = f32[512,11,32]{2,1,0:T(8,128)} reshape(f32[8,22528]{1,0:T(8,128)S(1)} %reduce) | data formatting | bytes 1441792
  56.5 3.1 %copy.95 = f32[11,32,8,64]{3,2,1,0:T(8,128)S(1)} copy(f32[11,32,8,64]{1,0,3,2:T(8,128)} %bitcast.67) | data formatting | bytes 1441792 | tf_op jit(solution)/shard_map/all_to_all | solution.py:34
  60.0 2.2 %convolution_bitcast_fusion.3 = f32[5,256,64]{1,2,0:T(8,128)S(1)} fusion(f32[5,256,64]{2,1,0:T(8,128)S(1)} %bitcast.75, s32[256]{0:T(256)S(1)} %and_select_fusion, f32[256]{0:T(256)S(1)} %broadcast_select_fusion, pred[256]{0:T(512)(128)(4,1)S(1)} %get-tuple-element.23, pred[256]{0:T(512)(128)(4,1)S(1)} %get-tuple-element.22, ...), kind=kOutput, calls=%fused_computation.8 | convolution fusion | flops 252903424 | bytes 658176 | tf_op jit(solution)/shard_map/tk,fkp->ftp/dot_general | solution.py:91
  62.2 2.2 %fusion.4 = f32[256,64]{0,1:T(8,128)S(1)} fusion(f32[5,256,64]{1,2,0:T(8,128)S(1)} %convolution_bitcast_fusion.3, f32[5,256,64]{2,1,0:T(8,128)S(1)} %bitcast.76, s32[256]{0:T(256)S(1)} %and_select_fusion, f32[256]{0:T(256)S(1)} %broadcast_select_fusion, pred[256]{0:T(512)(128)(4,1)S(1)} %get-tuple-element.23, pred[256]{0:T(512)(128)(4,1)S(1)} %get-tuple-element.22, ...), kind=kOutput, calls=%fused_computation.10 | convolution fusion | flops 253050880 | bytes 723712 | tf_op jit(solution)/shard_map/tk,fkp->ftp/dot_general | solution.py:92
  64.6 2.5 %convolution_bitcast_fusion.2 = f32[5,256,64]{1,2,0:T(8,128)S(1)} fusion(f32[5,256,64]{1,2,0:T(8,128)} %copy-done.6, f32[256,64]{0,1:T(8,128)S(1)} %copy.73, s32[256]{0:T(256)S(1)} %and_select_fusion, f32[256]{0:T(256)S(1)} %broadcast_select_fusion, pred[256]{0:T(512)(128)(4,1)S(1)} %get-tuple-element.23, pred[256]{0:T(512)(128)(4,1)S(1)} %get-tuple-element.22, ...), kind=kOutput, calls=%fused_computation.7 | convolution fusion | flops 252985344 | bytes 723712 | tf_op jit(solution)/shard_map/tk,ftp->fkp/dot_general | solution.py:94
  67.2 0.4 copy.78
  67.6 1.3 %reshape.159 = f32[8,1,12288]{2,1,0:T(1,128)} reshape(f32[256,6,64]{2,1,0:T(8,128)S(1)} %bitcast.72) | data formatting | bytes 786432
  68.9 4.8 %all-to-all-start.1 = ((f32[8,1,12288]{2,1,0:T(1,128)}), f32[8,1,12288]{2,1,0:T(1,128)}, u32[]{:S(2)}, u32[]{:S(2)}) async-start(f32[8,1,12288]{2,1,0:T(1,128)} %reshape.159), calls=%async_computation.1 | async-start | bytes 786432 | tf_op jit(solution)/shard_map/all_to_all | solution.py:34
  73.7 0.8 convolution_add_fusion.1
  74.5 0.8 fusion.2
  75.3 7.5 %all-to-all-done.1 = f32[8,1,12288]{2,1,0:T(1,128)} async-done(((f32[8,1,12288]{2,1,0:T(1,128)}), f32[8,1,12288]{2,1,0:T(1,128)}, u32[]{:S(2)}, u32[]{:S(2)}) %all-to-all-start.1) | async-done | bytes 393248 | tf_op jit(solution)/shard_map/all_to_all | solution.py:34
  82.8 2.6 %reduce.1 = f32[8,12288]{1,0:T(8,128)S(1)} reduce(f32[8,1,12288]{2,1,0:T(1,128)} %all-to-all-done.1, f32[]{:T(128)} %broadcast.226), dimensions={1}, to_apply=%all_to_all.25.reduce_sub_computation | reduce | bytes 786436 | tf_op jit(solution)/shard_map/all_to_all | solution.py:34
  86.6 0.8 fusion
  87.3 0.8 copy.84
  88.2 0.7 reshape.150
  (46 shorter events, 2.7 us)
Async XLA Ops:
  0.6 1.0 %copy-start = (f32[5,32,4,128]{3,2,1,0:T(4,128)S(1)}, f32[5,32,4,128]{3,2,1,0:T(4,128)}, u32[]{:S(2)}) copy-start(f32[5,32,4,128]{3,2,1,0:T(4,128)} %param.8) | copy-start | bytes 983044
  9.0 8.9 %copy-start.1 = (f32[5,32,4,128]{3,2,1,0:T(4,128)S(1)}, f32[5,32,4,128]{3,2,1,0:T(4,128)}, u32[]{:S(2)}) copy-start(f32[5,32,4,128]{3,2,1,0:T(4,128)} %param.7) | copy-start | bytes 983044
  13.4 35.9 %copy-start.3 = (f32[5,5]{1,0:T(8,128)S(1)}, f32[5,5]{1,0:T(8,128)}, u32[]{:S(2)}) copy-start(f32[5,5]{1,0:T(8,128)} %param.10) | copy-start | bytes 304
  13.4 36.7 %all-to-all-start = ((f32[8,1,22528]{2,1,0:T(1,128)}), f32[8,1,22528]{2,1,0:T(1,128)S(1)}, u32[]{:S(2)}, u32[]{:S(2)}) async-start(f32[8,1,22528]{2,1,0:T(1,128)} %reshape.157), calls=%async_computation | async-start | bytes 1441792 | tf_op jit(solution)/shard_map/all_to_all | solution.py:34
  18.8 20.1 %collective-permute-start.2 = (f32[5,32,4,1]{3,2,1,0:T(4,128)}, f32[5,32,4,1]{3,2,1,0:T(4,128)S(1)}, u32[]{:S(2)}, u32[]{:S(2)}) collective-permute-start(f32[5,32,4,1]{3,2,1,0:T(4,128)} %get-tuple-element.16), channel_id=1, source_target_pairs={{1,0},{3,2},{5,4},{7,6},{9,8},{11,10},{13,12},{15,14},{17,16},{19,... | collective-permute-start | bytes 7688 | tf_op jit(solution)/shard_map/ppermute | solution.py:20
  20.1 18.8 %collective-permute-start.3 = (f32[5,32,4,1]{3,2,1,0:T(4,128)S(1)}, f32[5,32,4,1]{3,2,1,0:T(4,128)}, u32[]{:S(2)}, u32[]{:S(2)}) collective-permute-start(f32[5,32,4,1]{3,2,1,0:T(4,128)S(1)} %get-tuple-element.17), channel_id=1, source_target_pairs={{0,1},{2,3},{4,5},{6,7},{8,9},{10,11},{12,13},{14,15},{16,17},{18,... | collective-permute-start | bytes 7688 | tf_op jit(solution)/shard_map/ppermute | solution.py:19
  25.5 13.4 %collective-permute-start = (f32[5,32,1,128]{3,2,1,0:T(1,128)S(1)}, f32[5,32,1,128]{3,2,1,0:T(1,128)S(1)}, u32[]{:S(2)}, u32[]{:S(2)}) collective-permute-start(f32[5,32,1,128]{3,2,1,0:T(1,128)S(1)} %get-tuple-element.18), channel_id=1, source_target_pairs={{2,0},{4,2},{6,4},{8,6},{10,8},{12,10},{14,12},{16,14},{18,16},{20... | collective-permute-start | bytes 245768 | tf_op jit(solution)/shard_map/ppermute | solution.py:20
  36.3 10.6 %collective-permute-start.1 = (f32[5,32,1,128]{3,2,1,0:T(1,128)S(1)}, f32[5,32,1,128]{3,2,1,0:T(1,128)S(1)}, u32[]{:S(2)}, u32[]{:S(2)}) collective-permute-start(f32[5,32,1,128]{3,2,1,0:T(1,128)S(1)} %get-tuple-element.19), channel_id=1, source_target_pairs={{0,2},{2,4},{4,6},{6,8},{8,10},{10,12},{12,14},{14,16},{16,18},{18... | collective-permute-start | bytes 245768 | tf_op jit(solution)/shard_map/ppermute | solution.py:19
  62.2 2.3 %copy-start.6 = (f32[5,256,64]{1,2,0:T(8,128)}, f32[5,256,64]{1,2,0:T(8,128)S(1)}, u32[]{:S(2)}) copy-start(f32[5,256,64]{1,2,0:T(8,128)S(1)} %convolution_bitcast_fusion.3) | copy-start | bytes 983044
  62.2 11.5 %copy-start.4 = (f32[5,5]{1,0:T(8,128)S(1)}, f32[5,5]{1,0:T(8,128)}, u32[]{:S(2)}) copy-start(f32[5,5]{1,0:T(8,128)} %param.11) | copy-start | bytes 304
  64.5 10.0 %copy-start.5 = (f32[5,5]{1,0:T(8,128)S(1)}, f32[5,5]{1,0:T(8,128)}, u32[]{:S(2)}) copy-start(f32[5,5]{1,0:T(8,128)} %param.12) | copy-start | bytes 304
  68.9 13.9 %all-to-all-start.1 = ((f32[8,1,12288]{2,1,0:T(1,128)}), f32[8,1,12288]{2,1,0:T(1,128)}, u32[]{:S(2)}, u32[]{:S(2)}) async-start(f32[8,1,12288]{2,1,0:T(1,128)} %reshape.159), calls=%async_computation.1 | async-start | bytes 786432 | tf_op jit(solution)/shard_map/all_to_all | solution.py:34
  75.3 11.3 %copy-start.2 = (f32[5,5]{1,0:T(8,128)S(1)}, f32[5,5]{1,0:T(8,128)}, u32[]{:S(2)}) copy-start(f32[5,5]{1,0:T(8,128)} %param.13) | copy-start | bytes 304
where the time goes:
time: 89.6 us; the launch traced here: 89 us
  starting transfers between devices  28.5 us (32%)
  local copies, waits for them, and re-layouts  24.6 us (27%)
  waiting for transfers between devices  15.5 us (17%)
  matrix products  11.4 us (13%)
  other arithmetic  7.78 us (9%)
  between operations  1.08 us (1%)
    ppermute x2, starting transfers between devices, with_halo(): lax.ppermute(first, axis, [(b, a) for a, b in up])  12.1 us
    unnamed x19, local copies, waits for them, and re-layouts  11.5 us
    all_to_all x2, starting transfers between devices, in_one_piece(): lax.all_to_all(both, axis, split_axis=split_dim, concat_axis=concat_dim,...  9.23 us
    ppermute x2, waiting for transfers between devices, with_halo(): lax.ppermute(last, axis, up)  8 us
    all_to_all x2, waiting for transfers between devices, in_one_piece(): lax.all_to_all(both, axis, split_axis=split_dim, concat_axis=concat_dim,...  7.5 us
    ppermute x2, starting transfers between devices, with_halo(): lax.ppermute(last, axis, up)  7.21 us
    all_to_all x2, other arithmetic, in_one_piece(): lax.all_to_all(both, axis, split_axis=split_dim, concat_axis=concat_dim,...  4.93 us
    concatenate x2, local copies, waits for them, and re-layouts, in_one_piece(): both = jnp.concatenate(arrays, axis=along)  4.06 us
  transfers between devices with their start and end apart: 6, of which 2 were waited for; matrix products, arithmetic and copies ran while one was open for 7% of the time, Pallas kernels for 0%

commit v1 on v0

v1 whole, which is shorter than its diff:
```python
import functools
import math

import jax
import jax.numpy as jnp
import ml_dtypes
import numpy as np
from jax import lax
from jax.experimental import pallas as pl
from jax.experimental.pallas import tpu as pltpu
from jax.sharding import PartitionSpec as P

MESH = pl.DeviceIdType.MESH
F, K, X, L = 5, 32, 4, 128
D = 8
HALF = L // 2
PAIRS = 3
ORDER = (4, 5, 3, 2, 6, 7, 1)


def basis_parts():
    t = np.arange(D * K)[:, None]
    k = np.arange(D * K)[None, :]
    phase = ((k // 2) * t % (D * K)) * (2.0 * math.pi / (D * K))
    table = math.sqrt(2.0 / (D * K)) * np.where(k % 2 == 0, np.cos(phase), np.sin(phase))
    one = 1.0 / math.sqrt(D * K)
    table = np.where(k == 0, one, table)
    table = np.where(k == 1, np.where(t % 2 == 0, one, -one), table)
    high = table.astype(ml_dtypes.bfloat16)
    low = (table - high.astype(np.float64)).astype(ml_dtypes.bfloat16)
    return high, low


def product(high, low, x):
    x_high = x.astype(jnp.bfloat16)
    x_low = (x - x_high.astype(jnp.float32)).astype(jnp.bfloat16)
    dot = functools.partial(jnp.dot, preferred_element_type=jnp.float32)
    return dot(high, x_high) + (dot(high, x_low) + dot(low, x_high))


def kernel(
    adj_ref, state_ref, wake_ref, bh_ref, bl_ref, th_ref, tl_ref, ja_ref, jr_ref, js_ref, wc_ref,
    out_ref, grad_ref,
    send, recv, wsend, wrecv, wfull, back, ret, hsend, hrecv, esend, erecv, acc,
    f_ssem, f_rsem, w_ssem, w_rsem, b_ssem, b_rsem, h_ssem, h_rsem, e_ssem, e_rsem,
):
    me = lax.axis_index("mode")
    ax = lax.axis_index("ax")
    rad = lax.axis_index("rad")
    ax_count = lax.axis_size("ax")
    ax_up = lax.rem(ax + 1, ax_count)
    ax_down = lax.rem(ax + ax_count - 1, ax_count)
    others = [lax.rem(me + i, D) for i in ORDER]

    barrier = pltpu.get_barrier_semaphore()
    for other in others:
        pl.semaphore_signal(barrier, inc=1, device_id={"mode": other}, device_id_type=MESH)
    pl.semaphore_signal(barrier, inc=1, device_id={"ax": ax_up}, device_id_type=MESH)
    pl.semaphore_signal(barrier, inc=1, device_id={"ax": ax_down}, device_id_type=MESH)
    pl.semaphore_signal(barrier, inc=1, device_id={"rad": 1 - rad}, device_id_type=MESH)

    lane = lax.broadcasted_iota(jnp.int32, (K, L), 1)
    low_half = lane < HALF

    def cells(ref, f, x):
        return ref[f, pl.ds(x, K, stride=X), :]

    def swap(v):
        return pltpu.roll(v, HALF, axis=1)

    edge = jnp.zeros((K, L), jnp.float32)
    for f in range(F):
        hsend[0, f] = cells(adj_ref, f, 0)
        hsend[1, f] = cells(adj_ref, f, X - 1)
        for x in range(X):
            s = f * X + x
            v = cells(adj_ref, f, x)
            v = jnp.where(rad == 0, pltpu.roll(v, s + 1, axis=1), pltpu.roll(v, s, axis=1) if s else v)
            edge = jnp.where(lane == s, v, edge)
    esend[...] = edge

    q = K // 2
    for x in range(X):
        w = wake_ref[pl.ds(x, K, stride=X), :]
        w_swap = swap(w)
        m = low_half[:q]
        wsend[2 * x] = jnp.where(m, w[:q], w_swap[q:])
        wsend[2 * x + 1] = jnp.where(m, w_swap[:q], w[q:])
        states = [cells(state_ref, e, x) for e in range(F)]
        for f in range(F):
            a = cells(adj_ref, f, x)
            c = wc_ref[f, 0] * states[0]
            for e in range(1, F):
                c = c + wc_ref[f, e] * states[e]
            send[f, 2 * x] = jnp.where(low_half, a, swap(c))
            send[f, 2 * x + 1] = jnp.where(low_half, swap(a), c)

    pl.semaphore_wait(barrier, D + 2)

    started = []

    def go(src, dst, ssem, rsem, device):
        copy = pltpu.make_async_remote_copy(
            src_ref=src, dst_ref=dst, send_sem=ssem, recv_sem=rsem, device_id=device, device_id_type=MESH
        )
        copy.start()
        started.append(copy)

    go(hsend.at[0], hrecv.at[1], h_ssem.at[0], h_rsem.at[1], {"ax": ax_down})
    go(hsend.at[1], hrecv.at[0], h_ssem.at[1], h_rsem.at[0], {"ax": ax_up})
    go(esend, erecv, e_ssem, e_rsem, {"rad": 1 - rad})
    for other in others:
        go(wsend.at[other], wrecv.at[me], w_ssem.at[other], w_rsem.at[me], {"mode": other})
    for f in range(F):
        for other in others:
            go(send.at[f, other], recv.at[f, me], f_ssem.at[f, other], f_rsem.at[f, me], {"mode": other})

    wrecv[me] = wsend[me]
    for f in range(F):
        recv[f, me] = send[f, me]

    def arrived(ref, sem):
        pltpu.make_async_remote_copy(
            src_ref=ref, dst_ref=ref, send_sem=sem, recv_sem=sem, device_id={"mode": me}, device_id_type=MESH
        ).wait_recv()

    for other in others:
        arrived(wrecv.at[other], w_rsem.at[other])
    for d in range(D):
        w = wrecv[d]
        w_swap = swap(w)
        m = low_half[:q]
        wfull[pl.ds(d * K, q), :] = jnp.where(m, w, w_swap)
        wfull[pl.ds(d * K + q, q), :] = jnp.where(m, w_swap, w)

    low_all = lax.broadcasted_iota(jnp.int32, (D * K, L), 1) < HALF
    total = None
    first = None
    for f in range(F):
        for other in others:
            arrived(recv.at[f, other], f_rsem.at[f, other])
        angle = product(bh_ref[...], bl_ref[...], recv[f].reshape(D * K, L))
        angle_swap = swap(angle)
        term = angle * angle_swap
        total = term if total is None else total + term
        wake_all = wfull[...]
        if f % 2 == 0 and f < F - 1:
            first = wake_all * angle
            continue
        p = f // 2
        if f < F - 1:
            both = jnp.where(low_all, first, wake_all * angle_swap)
        else:
            both = wake_all * angle
        result = product(th_ref[...], tl_ref[...], both)
        if f == F - 1:
            result = jnp.where(low_all, result, -total)
        back[p] = result.reshape(D, K, L)
        for other in others:
            go(back.at[p, other], ret.at[p, me], b_ssem.at[p, other], b_rsem.at[p, me], {"mode": other})
        ret[p, me] = back[p, me]

    arrived(hrecv.at[0], h_rsem.at[0])
    arrived(hrecv.at[1], h_rsem.at[1])
    arrived(erecv, e_rsem)
    row = lax.broadcasted_iota(jnp.int32, (K, L), 0)
    even = lax.rem(row, 2) == 0
    order = lax.div(me * K + row, 2).astype(jnp.float32) / jnp.float32(D * K // 2)
    radius = 0.5 + ((rad * L + lane).astype(jnp.float32) + 0.5) / jnp.float32(4.0 * L)
    rate = (0.25 / radius) * order
    rate = jnp.where(even, rate, -rate)
    nearby = erecv[...]
    nearby_up = jnp.where(rad == 0, nearby, 0.0)
    nearby_down = jnp.where(rad == 1, nearby, 0.0)
    for x in range(X):
        fields, axial, radial, turned = [], [], [], []
        for e in range(F):
            a = cells(adj_ref, e, x)
            fields.append(a)
            if x == X - 1:
                above = jnp.where(ax < ax_count - 1, hrecv[1, e], 0.0)
            else:
                above = cells(adj_ref, e, x + 1)
            if x == 0:
                below = jnp.where(ax > 0, hrecv[0, e], 0.0)
            else:
                below = cells(adj_ref, e, x - 1)
            axial.append(0.5 * (above - below))
            s = e * X + x
            up = jnp.where(lane == L - 1, pltpu.roll(nearby_up, L - 1 - s, axis=1), pltpu.roll(a, L - 1, axis=1))
            edge_down = pltpu.roll(nearby_down, L - s, axis=1) if s else nearby_down
            down = jnp.where(lane == 0, edge_down, pltpu.roll(a, 1, axis=1))
            radial.append(0.5 * (up - down))
            turned.append(rate * jnp.where(even, pltpu.roll(a, K - 1, axis=0), pltpu.roll(a, 1, axis=0)))
        for f in range(F):
            v = fields[f]
            for e in range(F):
                v = v + ja_ref[e, f] * axial[e] + jr_ref[e, f] * radial[e] + js_ref[e, f] * turned[e]
            acc[f, x] = v

    for p in range(PAIRS):
        for other in others:
            arrived(ret.at[p, other], b_rsem.at[p, other])
    for x in range(X):
        returned = []
        for p in range(PAIRS):
            one, two = ret[p, 2 * x], ret[p, 2 * x + 1]
            returned.append(jnp.where(low_half, one, swap(two)))
            returned.append(jnp.where(low_half, swap(one), two))
        grad_ref[pl.ds(x, K, stride=X), :] = returned[F]
        for f in range(F):
            v = acc[f, x]
            for e in range(F):
                v = v - wc_ref[e, f] * returned[e]
            out_ref[f, pl.ds(x, K, stride=X), :] = v

    for copy in started:
        copy.wait_send()


def body(adjoint, state, wake, jac_axial, jac_radial, jac_swirl, wake_coupling):
    high, low = basis_parts()
    vmem = pl.BlockSpec(memory_space=pltpu.VMEM)
    smem = pl.BlockSpec(memory_space=pltpu.SMEM)
    dma = pltpu.SemaphoreType.DMA
    f32 = jnp.float32
    adjoint_in, grad = pl.pallas_call(
        kernel,
        out_shape=(
            jax.ShapeDtypeStruct((F, K * X, L), f32),
            jax.ShapeDtypeStruct((K * X, L), f32),
        ),
        in_specs=[vmem] * 7 + [smem] * 4,
        out_specs=(vmem, vmem),
        scratch_shapes=[
            pltpu.VMEM((F, D, K, L), f32),
            pltpu.VMEM((F, D, K, L), f32),
            pltpu.VMEM((D, K // 2, L), f32),
            pltpu.VMEM((D, K // 2, L), f32),
            pltpu.VMEM((D * K, L), f32),
            pltpu.VMEM((PAIRS, D, K, L), f32),
            pltpu.VMEM((PAIRS, D, K, L), f32),
            pltpu.VMEM((2, F, K, L), f32),
            pltpu.VMEM((2, F, K, L), f32),
            pltpu.VMEM((K, L), f32),
            pltpu.VMEM((K, L), f32),
            pltpu.VMEM((F, X, K, L), f32),
            dma((F, D)), dma((F, D)), dma((D,)), dma((D,)), dma((PAIRS, D)), dma((PAIRS, D)),
            dma((2,)), dma((2,)), dma, dma,
        ],
        compiler_params=pltpu.CompilerParams(
            collective_id=0, has_side_effects=True, vmem_limit_bytes=32 * 1024 * 1024
        ),
        name="section_adjoint",
    )(
        adjoint.reshape(F, K * X, L), state.reshape(F, K * X, L), wake.reshape(K * X, L),
        jnp.asarray(high), jnp.asarray(low), jnp.asarray(np.ascontiguousarray(high.T)),
        jnp.asarray(np.ascontiguousarray(low.T)), jac_axial, jac_radial, jac_swirl, wake_coupling,
    )
    return adjoint_in.reshape(adjoint.shape), grad.reshape(wake.shape)


def solution(mesh):
    return jax.shard_map(
        body,
        mesh=mesh,
        in_specs=(
            P(None, "mode", "ax", "rad"),
            P(None, "mode", "ax", "rad"),
            P("mode", "ax", "rad"),
            P(),
            P(),
            P(),
            P(),
        ),
        out_specs=(P(None, "mode", "ax", "rad"), P("mode", "ax", "rad")),
        check_vma=False,
    )
```

time: 89.6 us -> 43.2 us (0.48)
  the two profiles are of different devices: /device:TPU:32 before, /device:TPU:1 now
where the time goes in v1:
time: 43.2 us; the launch traced here: 42.7 us
  Pallas kernels  31.6 us (73%)
  local copies, waits for them, and re-layouts  10.5 us (24%)
  between operations  0.66 us (2%)
    pallas_call x1, Pallas kernels, body(): pl.pallas_call(kernel, out_shape=(jax.ShapeDtypeStruct((F, K * X, L), f32...  31.6 us
    unnamed x24, local copies, waits for them, and re-layouts  10.5 us

profile of v1, /device:TPU:1, one launch (start us, length us, event | category | flops | bytes accessed | tf_op | source)
XLA Modules:
  0.0 42.7 jit_solution(5581871311300647595)
XLA Ops:
  0.6 0.0 copy-start.7
  0.6 0.7 %copy-done.7 = f32[5,5]{1,0:T(8,128)S(1)} copy-done((f32[5,5]{1,0:T(8,128)S(1)}, f32[5,5]{1,0:T(8,128)}, u32[]{:S(2)}) %copy-start.7) | copy-done | bytes 124
  1.3 0.0 copy-start
  1.3 1.0 %copy-done = f32[5,32,4,128]{3,2,1,0:T(4,128)S(1)} copy-done((f32[5,32,4,128]{3,2,1,0:T(4,128)S(1)}, f32[5,32,4,128]{3,2,1,0:T(4,128)}, u32[]{:S(2)}) %copy-start) | copy-done | bytes 327704
  2.3 0.0 copy-start.1
  2.3 1.0 %copy-done.1 = f32[5,32,4,128]{3,2,1,0:T(4,128)S(1)} copy-done((f32[5,32,4,128]{3,2,1,0:T(4,128)S(1)}, f32[5,32,4,128]{3,2,1,0:T(4,128)}, u32[]{:S(2)}) %copy-start.1) | copy-done | bytes 327704
  3.3 0.0 copy-start.2
  3.3 0.9 %copy-done.2 = bf16[256,256]{1,0:T(8,128)(2,1)S(1)} copy-done((bf16[256,256]{1,0:T(8,128)(2,1)S(1)}, bf16[256,256]{1,0:T(8,128)(2,1)}, u32[]{:S(2)}) %copy-start.2) | copy-done | bytes 131096
  4.2 0.0 copy-start.3
  4.2 0.9 %copy-done.3 = bf16[256,256]{1,0:T(8,128)(2,1)S(1)} copy-done((bf16[256,256]{1,0:T(8,128)(2,1)S(1)}, bf16[256,256]{1,0:T(8,128)(2,1)}, u32[]{:S(2)}) %copy-start.3) | copy-done | bytes 131096
  5.1 0.0 copy-start.4
  5.1 0.9 %copy-done.4 = bf16[256,256]{1,0:T(8,128)(2,1)S(1)} copy-done((bf16[256,256]{1,0:T(8,128)(2,1)S(1)}, bf16[256,256]{1,0:T(8,128)(2,1)}, u32[]{:S(2)}) %copy-start.4) | copy-done | bytes 131096
  6.0 0.0 copy-start.5
  6.0 0.9 %copy-done.5 = bf16[256,256]{1,0:T(8,128)(2,1)S(1)} copy-done((bf16[256,256]{1,0:T(8,128)(2,1)S(1)}, bf16[256,256]{1,0:T(8,128)(2,1)}, u32[]{:S(2)}) %copy-start.5) | copy-done | bytes 131096
  6.9 0.0 copy-start.6
  6.9 0.8 %copy-done.6 = f32[32,4,128]{2,1,0:T(4,128)S(1)} copy-done((f32[32,4,128]{2,1,0:T(4,128)S(1)}, f32[32,4,128]{2,1,0:T(4,128)}, u32[]{:S(2)}) %copy-start.6) | copy-done | bytes 65560
  7.7 0.0 copy-start.8
  7.7 0.7 %copy-done.8 = f32[5,5]{1,0:T(8,128)S(1)} copy-done((f32[5,5]{1,0:T(8,128)S(1)}, f32[5,5]{1,0:T(8,128)}, u32[]{:S(2)}) %copy-start.8) | copy-done | bytes 124
  8.4 0.0 copy-start.9
  8.4 0.7 %copy-done.9 = f32[5,5]{1,0:T(8,128)S(1)} copy-done((f32[5,5]{1,0:T(8,128)S(1)}, f32[5,5]{1,0:T(8,128)}, u32[]{:S(2)}) %copy-start.9) | copy-done | bytes 124
  9.1 0.0 copy-start.10
  9.1 0.7 %copy-done.10 = f32[5,5]{1,0:T(8,128)S(1)} copy-done((f32[5,5]{1,0:T(8,128)S(1)}, f32[5,5]{1,0:T(8,128)}, u32[]{:S(2)}) %copy-start.10) | copy-done | bytes 124
  9.8 31.6 %section_adjoint.1 = (f32[5,128,128]{2,1,0:T(8,128)S(1)}, f32[128,128]{1,0:T(8,128)S(1)}) custom-call(f32[5,128,128]{2,1,0:T(8,128)S(1)} %bitcast.6, f32[5,128,128]{2,1,0:T(8,128)S(1)} %bitcast.7, f32[128,128]{1,0:T(8,128)S(1)} %bitcast.8, bf16[256,256]{1,0:T(8,128)(2,1)S(1)} %copy-done.5, bf16[256,256]{1,0:T(8,128)(2,1)S(1)} %copy-done.4, ...), custom_call_target="tpu_custom_call" | custom-call | tf_op jit(solution)/shard_map/section_adjoint/pallas_call | solution.py:227
  41.4 0.7 %copy.15 = f32[5,32,4,128]{3,2,1,0:T(4,128)} copy(f32[5,32,4,128]{3,2,1,0:T(4,128)S(1)} %bitcast.5) | data formatting | bytes 655360
  42.1 0.6 %copy.16 = f32[32,4,128]{2,1,0:T(4,128)} copy(f32[32,4,128]{2,1,0:T(4,128)S(1)} %bitcast.9) | data formatting | bytes 131072
Async XLA Ops:
  0.6 0.7 %copy-start.7 = (f32[5,5]{1,0:T(8,128)S(1)}, f32[5,5]{1,0:T(8,128)}, u32[]{:S(2)}) copy-start(f32[5,5]{1,0:T(8,128)} %ja_ref.1) | copy-start | bytes 304
  1.3 1.0 %copy-start = (f32[5,32,4,128]{3,2,1,0:T(4,128)S(1)}, f32[5,32,4,128]{3,2,1,0:T(4,128)}, u32[]{:S(2)}) copy-start(f32[5,32,4,128]{3,2,1,0:T(4,128)} %param.11) | copy-start | bytes 983044
  2.3 1.0 %copy-start.1 = (f32[5,32,4,128]{3,2,1,0:T(4,128)S(1)}, f32[5,32,4,128]{3,2,1,0:T(4,128)}, u32[]{:S(2)}) copy-start(f32[5,32,4,128]{3,2,1,0:T(4,128)} %param.12) | copy-start | bytes 983044
  3.3 0.9 %copy-start.2 = (bf16[256,256]{1,0:T(8,128)(2,1)S(1)}, bf16[256,256]{1,0:T(8,128)(2,1)}, u32[]{:S(2)}) copy-start(bf16[256,256]{1,0:T(8,128)(2,1)} %constant.11.clone.tl_ref) | copy-start | bytes 393220
  4.2 0.9 %copy-start.3 = (bf16[256,256]{1,0:T(8,128)(2,1)S(1)}, bf16[256,256]{1,0:T(8,128)(2,1)}, u32[]{:S(2)}) copy-start(bf16[256,256]{1,0:T(8,128)(2,1)} %constant.10.clone.th_ref) | copy-start | bytes 393220
  5.1 0.9 %copy-start.4 = (bf16[256,256]{1,0:T(8,128)(2,1)S(1)}, bf16[256,256]{1,0:T(8,128)(2,1)}, u32[]{:S(2)}) copy-start(bf16[256,256]{1,0:T(8,128)(2,1)} %constant.9.clone.bl_ref) | copy-start | bytes 393220
  6.0 0.9 %copy-start.5 = (bf16[256,256]{1,0:T(8,128)(2,1)S(1)}, bf16[256,256]{1,0:T(8,128)(2,1)}, u32[]{:S(2)}) copy-start(bf16[256,256]{1,0:T(8,128)(2,1)} %constant.8.clone.bh_ref) | copy-start | bytes 393220
  6.9 0.8 %copy-start.6 = (f32[32,4,128]{2,1,0:T(4,128)S(1)}, f32[32,4,128]{2,1,0:T(4,128)}, u32[]{:S(2)}) copy-start(f32[32,4,128]{2,1,0:T(4,128)} %param.13) | copy-start | bytes 196612
  7.7 0.7 %copy-start.8 = (f32[5,5]{1,0:T(8,128)S(1)}, f32[5,5]{1,0:T(8,128)}, u32[]{:S(2)}) copy-start(f32[5,5]{1,0:T(8,128)} %jr_ref.1) | copy-start | bytes 304
  8.4 0.7 %copy-start.9 = (f32[5,5]{1,0:T(8,128)S(1)}, f32[5,5]{1,0:T(8,128)}, u32[]{:S(2)}) copy-start(f32[5,5]{1,0:T(8,128)} %js_ref.1) | copy-start | bytes 304
  9.1 0.7 %copy-start.10 = (f32[5,5]{1,0:T(8,128)S(1)}, f32[5,5]{1,0:T(8,128)}, u32[]{:S(2)}) copy-start(f32[5,5]{1,0:T(8,128)} %wc_ref.1) | copy-start | bytes 304
